TPU v7x, 256 devices: a whole 4x4x8 slice. The times are simulated.
256 devices in a mesh: pair: 8 (over x_lo, y), outv: 8 (over z), conv: 4 (over x_hi, core).
Axes of the slice: x: 4 (x_hi: 2, x_lo: 2; x = x_hi * 2 + x_lo), y: 4, z: 8, core: 2. Of those that a mesh axis runs over, the one named last changes fastest.
Arguments:
- amplitudes: bfloat16 [16384, 6144], P('pair', ('conv', 'outv')), may hold values from -6 to 6
- integrals: bfloat16 [6144, 12288], P('conv', ('outv', 'pair')), may hold values from -0.21875 to 0.21875
- amp_mask: int32 [8, 64], P('pair', 'conv'), may hold values from 0 to 1, as said below
- int_mask: int32 [64, 128], P('conv', 'outv'), may hold values 0 or 1
Outputs:
- ladder: bfloat16 [12288, 16384], P(('outv', 'conv'), 'pair')
Inputs may be any that keep to these rules, and one draw needn't show every extreme that they name: `amp_mask`: 0 or 1; the share of ones differs from pair tile to pair tile.
All inputs are finite; a program needn't handle non-finite values. No bound on the sum of `int_mask` on one device may be relied on, other than what follows from the above.
Results may differ from a plain program's by a relative error of at most 0.001.
Values may be sent and summed in bfloat16 or wider, within the bound.
No kernel may reach another device: no remote copies, remote signals or barrier semaphores. Data moves between devices by JAX's collectives and lax.ppermute only.
A program may use at most 64 MiB of HBM per device.

v0:
```python
import jax
import jax.numpy as jnp
from jax import lax
from jax.sharding import PartitionSpec as P

TW = 96


def column_mask(block_mask, first, width):
    tiles = block_mask.shape[1]
    col_tile = (first * width + jnp.arange(width, dtype=jnp.int32)) // TW
    onehot = (col_tile[None, :] == jnp.arange(tiles, dtype=jnp.int32)[:, None]).astype(jnp.float32)
    return jnp.dot(block_mask.astype(jnp.float32), onehot, preferred_element_type=jnp.float32)


def contract(columns, amp_rows):
    dims = (((0,), (1,)), ((), ()))
    return lax.dot_general(columns, amp_rows, dims, preferred_element_type=jnp.float32)


def body(amplitudes, integrals, amp_mask, int_mask):
    width_amp = amplitudes.shape[1]
    amp_cols = column_mask(amp_mask, lax.axis_index("outv"), width_amp)
    amp_local = amplitudes * amp_cols.astype(jnp.bfloat16)
    amp_rows = lax.all_gather(amp_local, "outv", axis=1, tiled=True)
    tiles_k = int_mask.shape[0]
    width_int = integrals.shape[1]
    int_cols = column_mask(int_mask, lax.axis_index("pair"), width_int)
    int_local = (
        integrals.reshape(tiles_k, TW, width_int) * int_cols[:, None, :].astype(jnp.bfloat16)
    ).reshape(tiles_k * TW, width_int)
    int_full = lax.all_gather(int_local, "pair", axis=1, tiled=True)
    summed = lax.psum_scatter(contract(int_full, amp_rows), "conv", scatter_dimension=0, tiled=True)
    return summed.astype(jnp.bfloat16)


def solution(mesh):
    placed = (
        P("pair", ("conv", "outv")),
        P("conv", ("outv", "pair")),
        P("pair", "conv"),
        P("conv", "outv"),
    )
    return jax.shard_map(
        body, mesh=mesh, in_specs=placed, out_specs=P(("outv", "conv"), "pair"), check_vma=False
    )
```

profile of v0, /device:TPU:1, one launch (start us, length us, event | category | flops | bytes accessed | tf_op | source)
XLA Modules:
  0.0 285.8 jit_solution(13967554948303165017)
XLA Ops:
  6.5 0.0 all-gather.3.cloned.1.call-start
  6.6 0.8 fusion
  7.4 0.1 copy.5
  7.5 0.5 mul.26
  8.0 0.9 mul.27
  8.9 2.0 mul.28
  10.9 0.0 all-gather.3.cloned.1.call-update
  10.9 0.0 all-gather.5.cloned.1.call-start
  11.0 0.8 fusion.1
  11.8 2.1 broadcast_multiply_fusion
  13.9 0.0 all-gather.5.cloned.1.call-update
  13.9 0.0 reduce-scatter.2.cloned.1.call-start
  14.0 61.0 %all-gather.3.cloned.1.call-done = bf16[1536,1536]{0,1:T(8,128)(2,1)} async-done(((bf16[1536,192]{0,1:T(8,128)(2,1)}), bf16[1536,1536]{0,1:T(8,128)(2,1)}) %all-gather.3.cloned.1.call-update) | async-done | bytes 4718608 | tf_op jit(solution)/shard_map/all_gather | solution.py:32
  75.0 75.1 %all-gather.5.cloned.1.call-done = bf16[2048,1536]{0,1:T(8,128)(2,1)} async-done(((bf16[2048,192]{0,1:T(8,128)(2,1)}), bf16[2048,1536]{0,1:T(8,128)(2,1)}) %all-gather.5.cloned.1.call-update) | async-done | bytes 6291472 | tf_op jit(solution)/shard_map/all_gather | solution.py:25
  150.1 16.1 %fusion.5 = f32[1536,2048]{1,0:T(8,128)} fusion(bf16[1536,1536]{0,1:T(8,128)(2,1)} %all-gather.3.cloned.1.call-done, bf16[2048,1536]{0,1:T(8,128)(2,1)} %all-gather.5.cloned.1.call-done), kind=kOutput, calls=%fused_computation.12 | convolution fusion | flops 9663676416 | bytes 23592960 | tf_op jit(solution)/shard_map/dot_general | solution.py:18
  166.2 0.0 reduce-scatter.2.cloned.1.call-update
  166.2 109.8 %reduce-scatter.2.cloned.1.call-done = f32[384,2048]{1,0:T(8,128)} async-done(((f32[1536,2048]{1,0:T(8,128)}), f32[384,2048]{1,0:T(8,128)}) %reduce-scatter.2.cloned.1.call-update) | async-done | bytes 3145744 | tf_op jit(solution)/shard_map/reduce_scatter | solution.py:33
  276.0 3.3 %convert_element_type.27 = bf16[384,2048]{1,0:T(8,128)(2,1)} convert(f32[384,2048]{1,0:T(8,128)} %reduce-scatter.2.cloned.1.call-done) | non-fusion elementwise | flops 786432 | bytes 4718592 | tf_op jit(solution)/shard_map/convert_element_type | solution.py:34
  (3 shorter events, 0.0 us)
Async XLA Ops:
  6.5 68.4 %all-gather.3.cloned.1.call-start = ((), (), s32[]{:S(2)}) async-start(), calls=%async_computation.1 | async-start | bytes 5308416 | tf_op jit(solution)/shard_map/all_gather | solution.py:32
  10.9 139.1 %all-gather.5.cloned.1.call-start = ((), (), s32[]{:S(2)}) async-start(), calls=%async_computation.2 | async-start | bytes 7077888 | tf_op jit(solution)/shard_map/all_gather | solution.py:25
  13.9 262.1 %reduce-scatter.2.cloned.1.call-start = ((), (), s32[]{:S(2)}) async-start(), calls=%async_computation.3 | async-start | bytes 15728640 | tf_op jit(solution)/shard_map/reduce_scatter | solution.py:33
Sparse Core Ops, SparseCore 0:
  11.0 63.8 all-gather.2
  76.7 73.2 all-gather.4
  166.3 109.6 reduce-scatter.1
where the time goes:
time: 286 us
  waiting for transfers between devices  246 us (86%)
  matrix products  17.7 us (6%)
  between operations  13.1 us (5%)
  other arithmetic  7.46 us (3%)
    reduce_scatter x1, waiting for transfers between devices, body(): lax.psum_scatter(contract(int_full, amp_rows), 'conv', scatter_dimension=...  110 us
    all_gather x1, waiting for transfers between devices, body(): amp_rows = lax.all_gather(amp_local, 'outv', axis=1, tiled=True)  75.1 us
    all_gather x1, waiting for transfers between devices, body(): int_full = lax.all_gather(int_local, 'pair', axis=1, tiled=True)  61 us
    dot_general x1, matrix products, contract(): lax.dot_general(columns, amp_rows, dims, preferred_element_type=jnp.float32)  16.1 us
  transfers between devices with their start and end apart: 3, of which 3 were waited for; matrix products, arithmetic and copies ran while one was open for 1% of the time, Pallas kernels for 0%

commit v1 on v0

--- a/solution.py
+++ b/solution.py
@@ -4,6 +4,12 @@
 from jax.sharding import PartitionSpec as P
 
 TW = 96
+
+
+def in_order(parts, dim):
+    parts = jnp.moveaxis(parts, 0, dim)
+    dims = parts.shape
+    return parts.reshape(*dims[:dim], dims[dim] * dims[dim + 1], *dims[dim + 2 :])
 
 
 def column_mask(block_mask, first, width):
@@ -22,7 +28,19 @@
     width_amp = amplitudes.shape[1]
     amp_cols = column_mask(amp_mask, lax.axis_index("outv"), width_amp)
     amp_local = amplitudes * amp_cols.astype(jnp.bfloat16)
-    amp_rows = lax.all_gather(amp_local, "outv", axis=1, tiled=True)
+    count = lax.axis_size("outv")
+    pairs = [(i, (i + 1) % count) for i in range(count)]
+    back = [(b, a) for a, b in pairs]
+    lower, upper = ([], [])
+    for lap in range(count - 1):
+        if lap % 2 == 0:
+            lower.append(lax.ppermute(lower[-1] if lower else amp_local, "outv", pairs))
+        else:
+            upper.append(lax.ppermute(upper[-1] if upper else amp_local, "outv", back))
+    blocks = jnp.stack([*lower[::-1], amp_local, *upper])
+    shift = lax.axis_index("outv") - len(lower)
+    blocks = blocks[(jnp.arange(count) - shift) % count]
+    amp_rows = in_order(blocks, 1)
     tiles_k = int_mask.shape[0]
     width_int = integrals.shape[1]
     int_cols = column_mask(int_mask, lax.axis_index("pair"), width_int)

time: 286 us -> 250 us (0.87)
  waiting for transfers between devices: 246 us -> 182 us
  local copies, waits for them, and re-layouts: 1.48 us -> 17.9 us
  starting transfers between devices: 0.09 us -> 10.9 us
    all_gather x1 -> x0, waiting for transfers between devices: 75.1 us -> none  [body(): amp_rows = lax.all_gather(amp_local, 'outv', axis=1, tiled=True)]
    ppermute x0 -> x7, waiting for transfers between devices: none -> 68.3 us  [the longest x4 68.3 us: body(): lower.append(lax.ppermute(lower[-1] if lower else amp_local, 'outv', pairs))]
    all_gather x1, waiting for transfers between devices: 61 us -> 0.01 us  [body(): int_full = lax.all_gather(int_local, 'pair', axis=1, tiled=True)]
    ppermute x0 -> x7, starting transfers between devices: none -> 10.8 us  [the longest x3 8.28 us: body(): upper.append(lax.ppermute(upper[-1] if upper else amp_local, 'outv', back))]
    unnamed x0 -> x8, local copies, waits for them, and re-layouts: none -> 9.13 us
    gather x0 -> x1, local copies, waits for them, and re-layouts: none -> 6.32 us  [body(): blocks = blocks[(jnp.arange(count) - shift) % count]]
    reduce_scatter x1, waiting for transfers between devices: 110 us -> 113 us  [body(): lax.psum_scatter(contract(int_full, amp_rows), 'conv', scatter_dimension=...]
  transfers between devices with their start and end apart: 3 -> 9, of which waited for: 3 -> 5; matrix products, arithmetic and copies ran while one was open for 1% -> 8% of each run, Pallas kernels for 0% -> 0%
where the time goes in v1:
time: 250 us; the launch traced here: 249 us
  waiting for transfers between devices  182 us (73%)
  local copies, waits for them, and re-layouts  17.9 us (7%)
  matrix products  17.8 us (7%)
  between operations  13.5 us (5%)
  starting transfers between devices  10.9 us (4%)
  other arithmetic  7.68 us (3%)
    reduce_scatter x1, waiting for transfers between devices, body(): lax.psum_scatter(contract(int_full, amp_rows), 'conv', scatter_dimension=...  113 us
    ppermute x4, waiting for transfers between devices, body(): lower.append(lax.ppermute(lower[-1] if lower else amp_local, 'outv', pairs))  68.3 us
    dot_general x1, matrix products, contract(): lax.dot_general(columns, amp_rows, dims, preferred_element_type=jnp.float32)  16.2 us
    unnamed x8, local copies, waits for them, and re-layouts  9.13 us
    ppermute x3, starting transfers between devices, body(): upper.append(lax.ppermute(upper[-1] if upper else amp_local, 'outv', back))  8.28 us
    gather x1, local copies, waits for them, and re-layouts, body(): blocks = blocks[(jnp.arange(count) - shift) % count]  6.32 us
  transfers between devices with their start and end apart: 9, of which 5 were waited for; matrix products, arithmetic and copies ran while one was open for 8% of the time, Pallas kernels for 0%

profile of v1, /device:TPU:1, one launch (start us, length us, event | category | flops | bytes accessed | tf_op | source)
XLA Modules:
  0.0 249.4 jit_solution(7364283996512838495)
XLA Ops:
  6.5 0.0 copy-start
  6.5 0.0 all-gather.2.cloned.1.call-start
  6.6 0.9 fusion
  7.4 0.1 copy.5
  7.6 0.5 mul.26
  8.0 0.9 mul.27
  8.9 2.0 mul.28
  11.0 0.0 all-gather.2.cloned.1.call-update
  11.0 0.0 reduce-scatter.2.cloned.1.call-start
  11.1 0.8 fusion.1
  11.8 1.3 broadcast_multiply_fusion
  13.1 2.5 %collective-permute-start = (bf16[2048,192]{0,1:T(8,128)(2,1)S(1)}, bf16[2048,192]{0,1:T(8,128)(2,1)S(1)}, u32[]{:S(2)}, u32[]{:S(2)}) collective-permute-start(bf16[2048,192]{0,1:T(8,128)(2,1)S(1)} %broadcast_multiply_fusion), channel_id=1, source_target_pairs={{0,4},{4,8},{8,12},{12,16},{16,20},{20,24},{24,28},{28,0},{1,5},{5... | collective-permute-start | bytes 2359304 | tf_op jit(solution)/shard_map/ppermute | solution.py:37
  15.6 21.3 %collective-permute-done = bf16[2048,192]{0,1:T(8,128)(2,1)S(1)} collective-permute-done((bf16[2048,192]{0,1:T(8,128)(2,1)S(1)}, bf16[2048,192]{0,1:T(8,128)(2,1)S(1)}, u32[]{:S(2)}, u32[]{:S(2)}) %collective-permute-start) | collective-permute-done | bytes 786464 | tf_op jit(solution)/shard_map/ppermute | solution.py:37
  37.0 0.0 collective-permute-start.1
  37.0 2.7 %collective-permute-start.4 = (bf16[2048,192]{0,1:T(8,128)(2,1)S(1)}, bf16[2048,192]{0,1:T(8,128)(2,1)S(1)}, u32[]{:S(2)}, u32[]{:S(2)}) collective-permute-start(bf16[2048,192]{0,1:T(8,128)(2,1)S(1)} %broadcast_multiply_fusion), channel_id=1, source_target_pairs={{4,0},{8,4},{12,8},{16,12},{20,16},{24,20},{28,24},{0,28},{5,1},{9... | collective-permute-start | bytes 2359304 | tf_op jit(solution)/shard_map/ppermute | solution.py:39
  39.6 16.5 %collective-permute-done.1 = bf16[2048,192]{0,1:T(8,128)(2,1)S(1)} collective-permute-done((bf16[2048,192]{0,1:T(8,128)(2,1)S(1)}, bf16[2048,192]{0,1:T(8,128)(2,1)S(1)}, u32[]{:S(2)}, u32[]{:S(2)}) %collective-permute-start.1) | collective-permute-done | bytes 786464 | tf_op jit(solution)/shard_map/ppermute | solution.py:37
  56.2 0.0 collective-permute-start.2
  56.2 0.0 collective-permute-done.4
  56.2 2.7 %collective-permute-start.5 = (bf16[2048,192]{0,1:T(8,128)(2,1)S(1)}, bf16[2048,192]{0,1:T(8,128)(2,1)}, u32[]{:S(2)}, u32[]{:S(2)}) collective-permute-start(bf16[2048,192]{0,1:T(8,128)(2,1)S(1)} %collective-permute-done.4), channel_id=1, source_target_pairs={{4,0},{8,4},{12,8},{16,12},{20,16},{24,20},{28,24},{0,28},{5,1},{9... | collective-permute-start | bytes 2359304 | tf_op jit(solution)/shard_map/ppermute | solution.py:39
  58.9 15.7 %collective-permute-done.2 = bf16[2048,192]{0,1:T(8,128)(2,1)} collective-permute-done((bf16[2048,192]{0,1:T(8,128)(2,1)S(1)}, bf16[2048,192]{0,1:T(8,128)(2,1)}, u32[]{:S(2)}, u32[]{:S(2)}) %collective-permute-start.2) | collective-permute-done | bytes 786464 | tf_op jit(solution)/shard_map/ppermute | solution.py:37
  74.6 0.0 collective-permute-start.3
  74.6 0.0 collective-permute-done.5
  74.6 2.9 %collective-permute-start.6 = (bf16[2048,192]{0,1:T(8,128)(2,1)}, bf16[2048,192]{0,1:T(8,128)(2,1)S(1)}, u32[]{:S(2)}, u32[]{:S(2)}) collective-permute-start(bf16[2048,192]{0,1:T(8,128)(2,1)} %collective-permute-done.5), channel_id=1, source_target_pairs={{4,0},{8,4},{12,8},{16,12},{20,16},{24,20},{28,24},{0,28},{5,1},{9... | collective-permute-start | bytes 2359304 | tf_op jit(solution)/shard_map/ppermute | solution.py:39
  77.6 14.7 %collective-permute-done.3 = bf16[2048,192]{0,1:T(8,128)(2,1)} collective-permute-done((bf16[2048,192]{0,1:T(8,128)(2,1)}, bf16[2048,192]{0,1:T(8,128)(2,1)}, u32[]{:S(2)}, u32[]{:S(2)}) %collective-permute-start.3) | collective-permute-done | bytes 786464 | tf_op jit(solution)/shard_map/ppermute | solution.py:37
  92.3 2.1 bitcast_dynamic-update-slice_fusion.7
  94.4 2.1 bitcast_dynamic-update-slice_fusion.6
  96.5 0.9 bitcast_dynamic-update-slice_fusion.5
  97.4 0.9 bitcast_dynamic-update-slice_fusion.4
  98.4 0.0 copy-done
  98.4 1.1 bitcast_dynamic-update-slice_fusion.3
  99.5 0.9 bitcast_dynamic-update-slice_fusion.2
  100.4 2.1 bitcast_dynamic-update-slice_fusion.1
  102.5 0.0 collective-permute-done.6
  102.5 0.9 bitcast_dynamic-update-slice_fusion
  103.5 6.3 %gather_fusion = bf16[8,2048,192]{1,2,0:T(8,128)(2,1)} fusion(bf16[8,2048,192]{1,2,0:T(8,128)(2,1)} %bitcast_dynamic-update-slice_fusion, s32[1024]{0:T(1024)S(1)} %pad_clamp_fusion), kind=kCustom, calls=%fused_computation | custom fusion | bytes 12582944 | tf_op jit(solution)/shard_map/gather | solution.py:42
  109.8 0.0 all-gather.2.cloned.1.call-done
  109.8 16.2 %fusion.7 = f32[1536,2048]{1,0:T(8,128)} fusion(bf16[1536,1536]{0,1:T(8,128)(2,1)} %all-gather.2.cloned.1.call-done, bf16[2048,1536]{0,1:T(8,128)(2,1)} %bitcast.32), kind=kOutput, calls=%fused_computation.28 | convolution fusion | flops 9663676416 | bytes 23592960 | tf_op jit(solution)/shard_map/dot_general | solution.py:24
  125.9 0.0 reduce-scatter.2.cloned.1.call-update
  126.0 113.3 %reduce-scatter.2.cloned.1.call-done = f32[384,2048]{1,0:T(8,128)} async-done(((f32[1536,2048]{1,0:T(8,128)}), f32[384,2048]{1,0:T(8,128)}) %reduce-scatter.2.cloned.1.call-update) | async-done | bytes 3145744 | tf_op jit(solution)/shard_map/reduce_scatter | solution.py:51
  239.3 3.3 %convert_element_type.27 = bf16[384,2048]{1,0:T(8,128)(2,1)} convert(f32[384,2048]{1,0:T(8,128)} %reduce-scatter.2.cloned.1.call-done) | non-fusion elementwise | flops 786432 | bytes 4718592 | tf_op jit(solution)/shard_map/convert_element_type | solution.py:52
  (5 shorter events, 0.1 us)
Async XLA Ops:
  6.5 91.8 %copy-start = (bf16[2048,192]{0,1:T(8,128)(2,1)S(1)}, bf16[2048,192]{0,1:T(8,128)(2,1)}, u32[]{:S(2)}) copy-start(bf16[2048,192]{0,1:T(8,128)(2,1)} %param.4) | copy-start | bytes 2359300
  6.5 103.2 %all-gather.2.cloned.1.call-start = ((), (), s32[]{:S(2)}) async-start(), calls=%async_computation.1 | async-start | bytes 5308416 | tf_op jit(solution)/shard_map/all_gather | solution.py:50
  11.0 228.3 %reduce-scatter.2.cloned.1.call-start = ((), (), s32[]{:S(2)}) async-start(), calls=%async_computation.2 | async-start | bytes 15728640 | tf_op jit(solution)/shard_map/reduce_scatter | solution.py:51
  13.1 23.9 %collective-permute-start = (bf16[2048,192]{0,1:T(8,128)(2,1)S(1)}, bf16[2048,192]{0,1:T(8,128)(2,1)S(1)}, u32[]{:S(2)}, u32[]{:S(2)}) collective-permute-start(bf16[2048,192]{0,1:T(8,128)(2,1)S(1)} %broadcast_multiply_fusion), channel_id=1, source_target_pairs={{0,4},{4,8},{8,12},{12,16},{16,20},{20,24},{24,28},{28,0},{1,5},{5... | collective-permute-start | bytes 2359304 | tf_op jit(solution)/shard_map/ppermute | solution.py:37
  37.0 19.2 %collective-permute-start.1 = (bf16[2048,192]{0,1:T(8,128)(2,1)S(1)}, bf16[2048,192]{0,1:T(8,128)(2,1)S(1)}, u32[]{:S(2)}, u32[]{:S(2)}) collective-permute-start(bf16[2048,192]{0,1:T(8,128)(2,1)S(1)} %collective-permute-done), channel_id=1, source_target_pairs={{0,4},{4,8},{8,12},{12,16},{16,20},{20,24},{24,28},{28,0},{1,5},{5... | collective-permute-start | bytes 2359304 | tf_op jit(solution)/shard_map/ppermute | solution.py:37
  37.0 19.2 %collective-permute-start.4 = (bf16[2048,192]{0,1:T(8,128)(2,1)S(1)}, bf16[2048,192]{0,1:T(8,128)(2,1)S(1)}, u32[]{:S(2)}, u32[]{:S(2)}) collective-permute-start(bf16[2048,192]{0,1:T(8,128)(2,1)S(1)} %broadcast_multiply_fusion), channel_id=1, source_target_pairs={{4,0},{8,4},{12,8},{16,12},{20,16},{24,20},{28,24},{0,28},{5,1},{9... | collective-permute-start | bytes 2359304 | tf_op jit(solution)/shard_map/ppermute | solution.py:39
  56.2 18.4 %collective-permute-start.2 = (bf16[2048,192]{0,1:T(8,128)(2,1)S(1)}, bf16[2048,192]{0,1:T(8,128)(2,1)}, u32[]{:S(2)}, u32[]{:S(2)}) collective-permute-start(bf16[2048,192]{0,1:T(8,128)(2,1)S(1)} %collective-permute-done.1), channel_id=1, source_target_pairs={{0,4},{4,8},{8,12},{12,16},{16,20},{20,24},{24,28},{28,0},{1,5},{5... | collective-permute-start | bytes 2359304 | tf_op jit(solution)/shard_map/ppermute | solution.py:37
  56.2 18.4 %collective-permute-start.5 = (bf16[2048,192]{0,1:T(8,128)(2,1)S(1)}, bf16[2048,192]{0,1:T(8,128)(2,1)}, u32[]{:S(2)}, u32[]{:S(2)}) collective-permute-start(bf16[2048,192]{0,1:T(8,128)(2,1)S(1)} %collective-permute-done.4), channel_id=1, source_target_pairs={{4,0},{8,4},{12,8},{16,12},{20,16},{24,20},{28,24},{0,28},{5,1},{9... | collective-permute-start | bytes 2359304 | tf_op jit(solution)/shard_map/ppermute | solution.py:39
  74.6 17.7 %collective-permute-start.3 = (bf16[2048,192]{0,1:T(8,128)(2,1)}, bf16[2048,192]{0,1:T(8,128)(2,1)}, u32[]{:S(2)}, u32[]{:S(2)}) collective-permute-start(bf16[2048,192]{0,1:T(8,128)(2,1)} %collective-permute-done.2), channel_id=1, source_target_pairs={{0,4},{4,8},{8,12},{12,16},{16,20},{20,24},{24,28},{28,0},{1,5},{5... | collective-permute-start | bytes 2359304 | tf_op jit(solution)/shard_map/ppermute | solution.py:37
  74.6 27.9 %collective-permute-start.6 = (bf16[2048,192]{0,1:T(8,128)(2,1)}, bf16[2048,192]{0,1:T(8,128)(2,1)S(1)}, u32[]{:S(2)}, u32[]{:S(2)}) collective-permute-start(bf16[2048,192]{0,1:T(8,128)(2,1)} %collective-permute-done.5), channel_id=1, source_target_pairs={{4,0},{8,4},{12,8},{16,12},{20,16},{24,20},{28,24},{0,28},{5,1},{9... | collective-permute-start | bytes 2359304 | tf_op jit(solution)/shard_map/ppermute | solution.py:39
Sparse Core Ops, SparseCore 0:
  11.1 63.8 all-gather.1
  126.1 113.1 reduce-scatter.1
